TPU v7x, 32 devices: a whole 2x2x4 slice. The times are simulated.
32 devices in a mesh: dp: 8 (over z, x), tensor: 4 (over y, core).
Axes of the slice: x: 2, y: 2, z: 4, core: 2. Of those that a mesh axis runs over, the one named last changes fastest.
Arguments:
- hidden_in: bfloat16 [16, 1024, 1024], P('dp', 'tensor'), may hold values from -6 to 6
- out_grad: bfloat16 [16, 1024, 1024], P('dp', 'tensor'), may hold values from -6 to 6
- doc_ids: int32 [16, 1, 1024], P('dp'), may hold values from 0 to 2, never falling along the last dimension, each value on 1 to 512 neighbouring positions
- w_query: bfloat16 [1024, 1024], P('dp', 'tensor'), may hold values from -0.1875 to 0.1875
- w_key: bfloat16 [1024, 1024], P('dp', 'tensor'), may hold values from -0.1875 to 0.1875
- w_value: bfloat16 [1024, 1024], P('dp', 'tensor'), may hold values from -0.1875 to 0.1875
- w_output: bfloat16 [1024, 1024], P('tensor', 'dp'), may hold values from -0.1875 to 0.1875
- w_up: bfloat16 [1024, 4096], P('dp', 'tensor'), may hold values from -0.1875 to 0.1875
- w_gate: bfloat16 [1024, 4096], P('dp', 'tensor'), may hold values from -0.1875 to 0.1875
- w_down: bfloat16 [4096, 1024], P('tensor', 'dp'), may hold values from -0.09375 to 0.09375
- scale_qk: float32 [1024], P(('dp', 'tensor')), may hold values from 0.8 to 1.6
- alpha_attn: float32 [1024], P(('dp', 'tensor')), may hold values from 0.2 to 0.8
- alpha_mlp: float32 [1024], P(('dp', 'tensor')), may hold values from 0.2 to 0.8
- scale_up: float32 [4096], P(('dp', 'tensor')), may hold values from 0.5 to 2
- scale_gate: float32 [4096], P(('dp', 'tensor')), may hold values from 0.5 to 2
Outputs:
- layer_out: bfloat16 [16, 1024, 1024], P('dp', 'tensor')
- input_grad: bfloat16 [16, 1024, 1024], P('dp', 'tensor')
- grad_query: float32 [1024, 1024], P('dp', 'tensor')
- grad_key: float32 [1024, 1024], P('dp', 'tensor')
- grad_value: float32 [1024, 1024], P('dp', 'tensor')
- grad_output: float32 [1024, 1024], P('tensor', 'dp')
- grad_up: float32 [1024, 4096], P('dp', 'tensor')
- grad_gate: float32 [1024, 4096], P('dp', 'tensor')
- grad_down: float32 [4096, 1024], P('tensor', 'dp')
- grad_scale_qk: float32 [1024], P(('dp', 'tensor'))
- grad_alpha_attn: float32 [1024], P(('dp', 'tensor'))
- grad_alpha_mlp: float32 [1024], P(('dp', 'tensor'))
- grad_scale_up: float32 [4096], P(('dp', 'tensor'))
- grad_scale_gate: float32 [4096], P(('dp', 'tensor'))
Inputs may be any that keep to these rules, and one draw needn't show every extreme that they name: `doc_ids`: each sequence packs 3 documents of ids 0 to 2 in order, each of at most 512 tokens.
All inputs are finite; a program needn't handle non-finite values.
Results may differ from a plain program's by a relative error of at most 0.028.
Values may be sent and summed in bfloat16 or wider, within the bound.
A program may use at most 192 MiB of HBM per device.

v0:
```python
import math

import jax
import jax.numpy as jnp
from jax import lax
from jax.sharding import PartitionSpec as P

DH = 64
BLOCK = 256
DOCS = 3


def scattered(portion, extent, axis):
    count = extent * lax.axis_size(axis)
    sent = portion(jnp.int32(0), count).astype(jnp.bfloat16)
    return lax.psum_scatter(sent, axis, scatter_dimension=0, tiled=True).astype(jnp.float32)


def rms_scale(vals):
    return vals * lax.rsqrt(jnp.mean(vals * vals, axis=-1, keepdims=True) + 1e-06)


def unit_rows(vals):
    return vals * lax.rsqrt(jnp.sum(vals * vals, axis=-1, keepdims=True) + 1e-06)


def rotate(vals, cosine, sine):
    half = vals.shape[-1] // 2
    first = vals[..., :half]
    second = vals[..., half:]
    return jnp.concatenate(
        [first * cosine - second * sine, first * sine + second * cosine], axis=-1
    )


def prepare(raw, cosine, sine, gain):
    return gain * unit_rows(rotate(raw, cosine, sine))


def doc_places(docs):
    labels = jnp.arange(DOCS, dtype=jnp.int32)
    member = (docs[..., :, None] == labels).astype(jnp.int32)
    counts = jnp.sum(member, axis=-2)
    starts = jnp.cumsum(counts, axis=-1) - counts
    first = jnp.sum(member * starts[..., None, :], axis=-1)
    return jnp.arange(docs.shape[-1], dtype=jnp.int32) - first


def angles(places):
    steps = jnp.arange(DH // 2, dtype=jnp.float32) / (DH // 2)
    freqs = jnp.exp(-math.log(10000.0) * steps)
    turn = places.astype(jnp.float32)[..., None] * freqs
    return (jnp.cos(turn), jnp.sin(turn))


def block_scores(query_rows, keys, doc_row, blocks, low_row, score_scale):
    count = query_rows.shape[0]
    row_docs = doc_row[low_row : low_row + count]
    row_blocks = blocks[low_row : low_row + count]
    allowed = (row_docs[:, None] == doc_row[None, :]) & (blocks[None, :] <= row_blocks[:, None])
    scores = (
        jnp.einsum("qhd,khd->hqk", query_rows, keys, preferred_element_type=jnp.float32)
        * score_scale
    )
    return jnp.where(allowed[None], scores, -1e30)


def attend_forward(queries, keys, values, doc_row, block_rows, score_scale):
    blocks = doc_places(doc_row) // BLOCK
    outputs = []
    totals = []
    for block_index in range(doc_row.shape[0] // block_rows):
        low_row = block_index * block_rows
        scores = block_scores(
            queries[low_row : low_row + block_rows], keys, doc_row, blocks, low_row, score_scale
        )
        peak = jnp.max(scores, axis=-1, keepdims=True)
        expo = jnp.exp(scores - peak)
        total = jnp.sum(expo, axis=-1, keepdims=True)
        probs = (expo / total).astype(jnp.bfloat16)
        outputs.append(
            jnp.einsum("hqk,khd->qhd", probs, values, preferred_element_type=jnp.float32)
        )
        totals.append((peak + jnp.log(total))[..., 0])
    return (jnp.concatenate(outputs, axis=0), jnp.concatenate(totals, axis=1))


def attend_backward(queries, keys, values, grad_mixed, log_sums, doc_row, block_rows, score_scale):
    blocks = doc_places(doc_row) // BLOCK
    grad_keys = jnp.zeros(keys.shape, jnp.float32)
    grad_values = jnp.zeros(values.shape, jnp.float32)
    grad_queries = []
    for block_index in range(doc_row.shape[0] // block_rows):
        low_row = block_index * block_rows
        query_rows = queries[low_row : low_row + block_rows]
        grad_rows = grad_mixed[low_row : low_row + block_rows]
        scores = block_scores(query_rows, keys, doc_row, blocks, low_row, score_scale)
        probs = jnp.exp(scores - log_sums[:, low_row : low_row + block_rows, None])
        grad_probs = jnp.einsum(
            "qhd,khd->hqk", grad_rows, values, preferred_element_type=jnp.float32
        )
        inner = jnp.sum(grad_probs * probs, axis=-1, keepdims=True)
        grad_scores = (probs * (grad_probs - inner)).astype(jnp.bfloat16)
        grad_queries.append(
            jnp.einsum("hqk,khd->qhd", grad_scores, keys, preferred_element_type=jnp.float32)
            * score_scale
        )
        grad_keys = (
            grad_keys
            + jnp.einsum(
                "hqk,qhd->khd", grad_scores, query_rows, preferred_element_type=jnp.float32
            )
            * score_scale
        )
        grad_values = grad_values + jnp.einsum(
            "hqk,qhd->khd",
            probs.astype(jnp.bfloat16),
            grad_rows,
            preferred_element_type=jnp.float32,
        )
    return (jnp.concatenate(grad_queries, axis=0), grad_keys, grad_values)


def mix_step(rows_in, branch, alpha):
    return rms_scale(rows_in + alpha * (rms_scale(branch) - rows_in))


def shards(
    hidden_in,
    out_grad,
    doc_ids,
    w_query,
    w_key,
    w_value,
    w_output,
    w_up,
    w_gate,
    w_down,
    scale_qk,
    alpha_attn,
    alpha_mlp,
    scale_up,
    scale_gate,
):
    rank = lax.axis_index("tensor")
    full_q, full_k, full_v, full_o, full_u, full_g, full_d = (
        lax.all_gather(w_query, "dp", axis=0, tiled=True),
        lax.all_gather(w_key, "dp", axis=0, tiled=True),
        lax.all_gather(w_value, "dp", axis=0, tiled=True),
        lax.all_gather(w_output, "dp", axis=1, tiled=True),
        lax.all_gather(w_up, "dp", axis=0, tiled=True),
        lax.all_gather(w_gate, "dp", axis=0, tiled=True),
        lax.all_gather(w_down, "dp", axis=1, tiled=True),
    )
    all_qk, all_attn, all_mlp, all_up, all_gate = (
        lax.all_gather(scale_qk, ("dp", "tensor"), axis=0, tiled=True),
        lax.all_gather(alpha_attn, ("dp", "tensor"), axis=0, tiled=True),
        lax.all_gather(alpha_mlp, ("dp", "tensor"), axis=0, tiled=True),
        lax.all_gather(scale_up, ("dp", "tensor"), axis=0, tiled=True),
        lax.all_gather(scale_gate, ("dp", "tensor"), axis=0, tiled=True),
    )
    width = full_q.shape[0]
    local_width = full_q.shape[1]
    local_hidden = full_u.shape[1]
    heads_here = local_width // DH
    gain_qk = lax.dynamic_slice_in_dim(all_qk, rank * local_width, local_width).reshape(
        heads_here, DH
    )
    gain_up = lax.dynamic_slice_in_dim(all_up, rank * local_hidden, local_hidden)
    gain_gate = lax.dynamic_slice_in_dim(all_gate, rank * local_hidden, local_hidden)
    piece_rows = hidden_in.shape[1]
    seq_count = doc_ids.shape[1]
    seq_len = doc_ids.shape[2]
    block_rows = min(512, seq_len)
    score_scale = math.sqrt(DH)
    shaped = (seq_count, seq_len, heads_here, DH)
    full_hidden = all_up.shape[0]
    totals = tuple(
        (
            jnp.zeros(weight.shape, jnp.float32)
            for weight in (full_q, full_k, full_v, full_o, full_u, full_g, full_d)
        )
    )
    total_qk = jnp.zeros((width,), jnp.float32)
    total_attn = jnp.zeros((width,), jnp.float32)
    total_mlp = jnp.zeros((width,), jnp.float32)
    total_up = jnp.zeros((full_hidden,), jnp.float32)
    total_gate = jnp.zeros((full_hidden,), jnp.float32)
    outputs = []
    input_grads = []
    for batch_index in range(hidden_in.shape[0]):
        own_rows = hidden_in[batch_index]
        docs = doc_ids[batch_index]
        cosine, sine = angles(doc_places(docs))
        cosine = cosine[:, :, None, :]
        sine = sine[:, :, None, :]
        gathered = lax.all_gather(own_rows, "tensor", axis=0, tiled=True)
        query_raw = jnp.dot(gathered, full_q, preferred_element_type=jnp.float32).reshape(shaped)
        key_raw = jnp.dot(gathered, full_k, preferred_element_type=jnp.float32).reshape(shaped)
        values = (
            jnp.dot(gathered, full_v, preferred_element_type=jnp.float32)
            .astype(jnp.bfloat16)
            .reshape(shaped)
        )
        queries_f, pull_query = jax.vjp(
            lambda raw, gain: prepare(raw, cosine, sine, gain), query_raw, gain_qk
        )
        keys_f, pull_key = jax.vjp(
            lambda raw, gain: prepare(raw, cosine, sine, gain), key_raw, gain_qk
        )
        queries = queries_f.astype(jnp.bfloat16)
        keys = keys_f.astype(jnp.bfloat16)
        mixed, log_sums = lax.map(
            lambda items: attend_forward(
                items[0], items[1], items[2], items[3], block_rows, score_scale
            ),
            (queries, keys, values, docs),
        )
        mixed = mixed.astype(jnp.bfloat16).reshape(-1, local_width)
        attn_sum = scattered(
            lambda start, count: jnp.dot(
                lax.dynamic_slice_in_dim(mixed, start, count),
                full_o,
                preferred_element_type=jnp.float32,
            ),
            piece_rows,
            "tensor",
        )
        middle, pull_middle = jax.vjp(mix_step, own_rows.astype(jnp.float32), attn_sum, all_attn)
        mid_gathered = lax.all_gather(middle.astype(jnp.bfloat16), "tensor", axis=0, tiled=True)
        up_raw = jnp.dot(mid_gathered, full_u, preferred_element_type=jnp.float32)
        gate_raw = jnp.dot(mid_gathered, full_g, preferred_element_type=jnp.float32)
        up_scaled = up_raw * gain_up
        gate_scaled = gate_raw * gain_gate
        sigma = jax.nn.sigmoid(gate_scaled)
        inner = (up_scaled * (gate_scaled * sigma)).astype(jnp.bfloat16)
        mlp_sum = scattered(
            lambda start, count: jnp.dot(
                lax.dynamic_slice_in_dim(inner, start, count),
                full_d,
                preferred_element_type=jnp.float32,
            ),
            piece_rows,
            "tensor",
        )
        result, pull_end = jax.vjp(mix_step, middle, mlp_sum, all_mlp)
        outputs.append(result.astype(jnp.bfloat16))
        grad_mid_direct, grad_mlp, part_alpha_mlp = pull_end(
            out_grad[batch_index].astype(jnp.float32)
        )
        mlp_grad_all = lax.all_gather(grad_mlp.astype(jnp.bfloat16), "tensor", axis=0, tiled=True)
        grad_inner = jnp.dot(mlp_grad_all, full_d.T, preferred_element_type=jnp.float32)
        batch_down = jnp.dot(inner.T, mlp_grad_all, preferred_element_type=jnp.float32)
        grad_up_scaled = grad_inner * (gate_scaled * sigma)
        grad_gate_scaled = grad_inner * up_scaled * sigma * (1.0 + gate_scaled * (1.0 - sigma))
        part_up = jnp.sum(grad_up_scaled * up_raw, axis=0)
        part_gate = jnp.sum(grad_gate_scaled * gate_raw, axis=0)
        up_low = (grad_up_scaled * gain_up).astype(jnp.bfloat16)
        gate_low = (grad_gate_scaled * gain_gate).astype(jnp.bfloat16)
        batch_up = jnp.dot(mid_gathered.T, up_low, preferred_element_type=jnp.float32)
        batch_gate = jnp.dot(mid_gathered.T, gate_low, preferred_element_type=jnp.float32)
        back_middle = scattered(
            lambda start, count: jnp.dot(
                lax.dynamic_slice_in_dim(up_low, start, count),
                full_u.T,
                preferred_element_type=jnp.float32,
            )
            + jnp.dot(
                lax.dynamic_slice_in_dim(gate_low, start, count),
                full_g.T,
                preferred_element_type=jnp.float32,
            ),
            piece_rows,
            "tensor",
        )
        grad_rows_direct, grad_attn, part_alpha_attn = pull_middle(grad_mid_direct + back_middle)
        attn_grad_all = lax.all_gather(grad_attn.astype(jnp.bfloat16), "tensor", axis=0, tiled=True)
        grad_mixed = (
            jnp.dot(attn_grad_all, full_o.T, preferred_element_type=jnp.float32)
            .astype(jnp.bfloat16)
            .reshape(shaped)
        )
        batch_out = jnp.dot(mixed.T, attn_grad_all, preferred_element_type=jnp.float32)
        grad_queries, grad_keys, grad_values = lax.map(
            lambda items: attend_backward(
                items[0], items[1], items[2], items[3], items[4], items[5], block_rows, score_scale
            ),
            (queries, keys, values, grad_mixed, log_sums, docs),
        )
        grad_query_raw, part_qk_query = pull_query(grad_queries)
        grad_key_raw, part_qk_key = pull_key(grad_keys)
        query_low = grad_query_raw.reshape(-1, local_width).astype(jnp.bfloat16)
        key_low = grad_key_raw.reshape(-1, local_width).astype(jnp.bfloat16)
        value_low = grad_values.reshape(-1, local_width).astype(jnp.bfloat16)
        batch_query = jnp.dot(gathered.T, query_low, preferred_element_type=jnp.float32)
        batch_key = jnp.dot(gathered.T, key_low, preferred_element_type=jnp.float32)
        batch_value = jnp.dot(gathered.T, value_low, preferred_element_type=jnp.float32)
        back_rows = scattered(
            lambda start, count: jnp.dot(query_low, full_q.T, preferred_element_type=jnp.float32)
            + jnp.dot(key_low, full_k.T, preferred_element_type=jnp.float32)
            + jnp.dot(
                lax.dynamic_slice_in_dim(value_low, start, count),
                full_v.T,
                preferred_element_type=jnp.float32,
            ),
            piece_rows,
            "tensor",
        )
        input_grads.append((grad_rows_direct + back_rows).astype(jnp.bfloat16))
        total_qk = total_qk + lax.dynamic_update_slice_in_dim(
            jnp.zeros((width,), jnp.float32),
            (part_qk_query + part_qk_key).reshape(-1),
            rank * local_width,
            0,
        )
        total_attn = total_attn + part_alpha_attn
        total_mlp = total_mlp + part_alpha_mlp
        total_up = total_up + lax.dynamic_update_slice_in_dim(
            jnp.zeros((full_hidden,), jnp.float32), part_up, rank * local_hidden, 0
        )
        total_gate = total_gate + lax.dynamic_update_slice_in_dim(
            jnp.zeros((full_hidden,), jnp.float32), part_gate, rank * local_hidden, 0
        )
        totals = tuple(
            (
                prior + extra
                for prior, extra in zip(
                    totals,
                    (
                        batch_query,
                        batch_key,
                        batch_value,
                        batch_out,
                        batch_up,
                        batch_gate,
                        batch_down,
                    ),
                )
            )
        )
    totals = (
        lax.psum_scatter(totals[0], "dp", scatter_dimension=0, tiled=True),
        lax.psum_scatter(totals[1], "dp", scatter_dimension=0, tiled=True),
        lax.psum_scatter(totals[2], "dp", scatter_dimension=0, tiled=True),
        lax.psum_scatter(totals[3], "dp", scatter_dimension=1, tiled=True),
        lax.psum_scatter(totals[4], "dp", scatter_dimension=0, tiled=True),
        lax.psum_scatter(totals[5], "dp", scatter_dimension=0, tiled=True),
        lax.psum_scatter(totals[6], "dp", scatter_dimension=1, tiled=True),
    )
    grad_qk, grad_attn_step, grad_mlp_step, grad_up_scale, grad_gate_scale = (
        lax.psum_scatter(total_qk, ("dp", "tensor"), scatter_dimension=0, tiled=True),
        lax.psum_scatter(total_attn, ("dp", "tensor"), scatter_dimension=0, tiled=True),
        lax.psum_scatter(total_mlp, ("dp", "tensor"), scatter_dimension=0, tiled=True),
        lax.psum_scatter(total_up, ("dp", "tensor"), scatter_dimension=0, tiled=True),
        lax.psum_scatter(total_gate, ("dp", "tensor"), scatter_dimension=0, tiled=True),
    )
    return (
        jnp.stack(outputs),
        jnp.stack(input_grads),
        totals[0],
        totals[1],
        totals[2],
        totals[3],
        totals[4],
        totals[5],
        totals[6],
        grad_qk,
        grad_attn_step,
        grad_mlp_step,
        grad_up_scale,
        grad_gate_scale,
    )


def solution(mesh):
    in_specs = (
        P("dp", "tensor", None),
        P("dp", "tensor", None),
        P("dp", None, None),
        P("dp", "tensor"),
        P("dp", "tensor"),
        P("dp", "tensor"),
        P("tensor", "dp"),
        P("dp", "tensor"),
        P("dp", "tensor"),
        P("tensor", "dp"),
        P(("dp", "tensor")),
        P(("dp", "tensor")),
        P(("dp", "tensor")),
        P(("dp", "tensor")),
        P(("dp", "tensor")),
    )
    out_specs = (
        P("dp", "tensor", None),
        P("dp", "tensor", None),
        P("dp", "tensor"),
        P("dp", "tensor"),
        P("dp", "tensor"),
        P("tensor", "dp"),
        P("dp", "tensor"),
        P("dp", "tensor"),
        P("tensor", "dp"),
        P(("dp", "tensor")),
        P(("dp", "tensor")),
        P(("dp", "tensor")),
        P(("dp", "tensor")),
        P(("dp", "tensor")),
    )
    return jax.shard_map(shards, mesh=mesh, in_specs=in_specs, out_specs=out_specs, check_vma=False)
```

profile of v0, /device:TPU:0, one launch (start us, length us, event | category | flops | bytes accessed | tf_op | source)
XLA Modules:
  0.0 1381.8 jit_solution(15086006827104064838)
XLA Ops:
  16.0 43.3 %all-reduce.17 = (f32[1024]{0:T(1024)S(1)}, f32[1024]{0:T(1024)S(1)}, f32[1024]{0:T(1024)S(1)}) all-reduce(f32[1024]{0:T(1024)S(1)} %dynamic-update-slice.4, f32[1024]{0:T(1024)S(1)} %dynamic-update-slice.3, f32[1024]{0:T(1024)S(1)} %dynamic-update-slice.5), channel_id=1, replica_groups=mesh['dp'=8,'tensor'=4] {'dp','tensor'}, use_global_device_ids=true, to_apply=%add.9 | all-reduce | flops 3072 | bytes 24576
  60.5 31.5 %all_gather.64 = bf16[1024,256]{1,0:T(8,128)(2,1)S(1)} all-gather(bf16[128,256]{1,0:T(8,128)(2,1)} %param.18), channel_id=1, replica_groups=mesh['dp'=8,'tensor'=4] {'dp'}, dimensions={0}, use_global_device_ids=true | all-gather | bytes 589824 | tf_op jit(solution)/shard_map/all_gather | solution.py:147
  92.0 31.7 %all_gather.65 = bf16[1024,256]{1,0:T(8,128)(2,1)S(1)} all-gather(bf16[128,256]{1,0:T(8,128)(2,1)} %param.19), channel_id=1, replica_groups=mesh['dp'=8,'tensor'=4] {'dp'}, dimensions={0}, use_global_device_ids=true | all-gather | bytes 589824 | tf_op jit(solution)/shard_map/all_gather | solution.py:148
  123.7 33.7 %all_gather.62 = bf16[1024,256]{1,0:T(8,128)(2,1)} all-gather(bf16[128,256]{1,0:T(8,128)(2,1)S(1)} %copy-done.114), channel_id=1, replica_groups=mesh['dp'=8,'tensor'=4] {'dp'}, dimensions={0}, use_global_device_ids=true | all-gather | bytes 589824 | tf_op jit(solution)/shard_map/all_gather | solution.py:149
  157.5 28.3 %all_gather.66 = bf16[256,1024]{1,0:T(8,128)(2,1)} all-gather(bf16[256,128]{1,0:T(8,128)(2,1)S(1)} %copy-done.115), channel_id=1, replica_groups=mesh['dp'=8,'tensor'=4] {'dp'}, dimensions={1}, use_global_device_ids=true | all-gather | bytes 589824 | tf_op jit(solution)/shard_map/all_gather | solution.py:150
  195.7 2.7 fusion.34
  220.9 29.4 %reduce-scatter.16.cloned.1.call-done = bf16[256,1024]{1,0:T(8,128)(2,1)} async-done(((bf16[1024,1024]{1,0:T(8,128)(2,1)}), bf16[256,1024]{1,0:T(8,128)(2,1)}) %reduce-scatter.16.cloned.1.call-update) | async-done | bytes 524304 | tf_op jit(solution)/shard_map/reduce_scatter | solution.py:16
  256.7 40.8 %all-gather.2 = f32[32,1,128]{2,1,0:T(1,128)S(1)} all-gather(f32[1,1,128]{2,1,0:T(1,128)S(1)} %bitcast.408), channel_id=1, replica_groups=mesh['dp'=8,'tensor'=4] {'dp','tensor'}, dimensions={0}, use_global_device_ids=true | all-gather | bytes 16896 | tf_op jit(solution)/shard_map/all_gather | solution.py:159
  297.5 37.0 %all-gather.3 = f32[32,1,128]{2,1,0:T(1,128)S(1)} all-gather(f32[1,1,128]{2,1,0:T(1,128)S(1)} %bitcast.409), channel_id=1, replica_groups=mesh['dp'=8,'tensor'=4] {'dp','tensor'}, dimensions={0}, use_global_device_ids=true | all-gather | bytes 16896 | tf_op jit(solution)/shard_map/all_gather | solution.py:160
  334.5 6.6 fusion.157
  341.1 3.7 all-gather.18.cloned.1.call-done
  344.8 8.9 multiply_convert_fusion.9
  353.7 42.3 %all-gather.22.cloned.1.call-done = bf16[1024,1024]{1,0:T(8,128)(2,1)} async-done(((bf16[1024,128]{1,0:T(8,128)(2,1)}), bf16[1024,1024]{1,0:T(8,128)(2,1)}) %all-gather.22.cloned.1.call-update) | async-done | bytes 2097168 | tf_op jit(solution)/shard_map/all_gather | solution.py:153
  395.9 6.0 convolution_convert_fusion.2
  405.7 5.3 fusion.156
  413.6 17.8 %reduce-scatter.18.cloned.1.call-done = bf16[256,1024]{1,0:T(8,128)(2,1)} async-done(((bf16[1024,1024]{1,0:T(8,128)(2,1)}), bf16[256,1024]{1,0:T(8,128)(2,1)}) %reduce-scatter.18.cloned.1.call-update) | async-done | bytes 524304 | tf_op jit(solution)/shard_map/reduce_scatter | solution.py:16
  432.7 2.4 fusion.94
  435.1 2.5 fusion.106
  441.5 4.5 fusion.2
  446.1 5.6 fusion.90
  457.0 5.2 all-gather.26.cloned.1.call-done
  462.2 10.5 multiply_reduce_fusion.5
  475.9 3.7 add_convert_fusion.3
  479.7 8.6 reduce-scatter.20.cloned.1.call-done
  489.6 32.4 %reduce-scatter.24.cloned.1.call-done = bf16[256,1024]{1,0:T(8,128)(2,1)} async-done(((bf16[1024,1024]{1,0:T(8,128)(2,1)}), bf16[256,1024]{1,0:T(8,128)(2,1)}) %reduce-scatter.24.cloned.1.call-update) | async-done | bytes 524304 | tf_op jit(solution)/shard_map/reduce_scatter | solution.py:16
  521.9 3.6 multiply_reduce_fusion.9
  527.1 22.3 %all-gather.24.cloned.1.call-done = bf16[1024,1024]{1,0:T(8,128)(2,1)} async-done(((bf16[256,1024]{1,0:T(8,128)(2,1)}), bf16[1024,1024]{1,0:T(8,128)(2,1)}) %all-gather.24.cloned.1.call-update) | async-done | bytes 2097168 | tf_op jit(solution)/shard_map/all_gather | solution.py:230
  549.4 4.7 fusion.158
  554.1 4.8 multiply_convert_fusion.8
  560.3 3.7 convolution_convert_fusion
  564.1 31.3 %reduce-scatter.22.cloned.1.call-done = bf16[256,1024]{1,0:T(8,128)(2,1)} async-done(((bf16[1024,1024]{1,0:T(8,128)(2,1)}), bf16[256,1024]{1,0:T(8,128)(2,1)}) %reduce-scatter.22.cloned.1.call-update) | async-done | bytes 524304 | tf_op jit(solution)/shard_map/reduce_scatter | solution.py:16
  598.9 2.5 fusion.111
  603.9 22.3 %all-gather.30.cloned.1.call-done = bf16[1024,1024]{1,0:T(8,128)(2,1)} async-done(((bf16[256,1024]{1,0:T(8,128)(2,1)}), bf16[1024,1024]{1,0:T(8,128)(2,1)}) %all-gather.30.cloned.1.call-update) | async-done | bytes 2097168 | tf_op jit(solution)/shard_map/all_gather | solution.py:251
  626.1 9.8 multiply_reduce_fusion.4
  639.1 3.7 add_convert_fusion.1
  642.9 31.2 %reduce-scatter.28.cloned.1.call-done = bf16[256,1024]{1,0:T(8,128)(2,1)} async-done(((bf16[1024,1024]{1,0:T(8,128)(2,1)}), bf16[256,1024]{1,0:T(8,128)(2,1)}) %reduce-scatter.28.cloned.1.call-update) | async-done | bytes 524304 | tf_op jit(solution)/shard_map/reduce_scatter | solution.py:16
  674.1 3.7 multiply_reduce_fusion.11
  682.8 21.9 %all-gather.32.cloned.1.call-done = bf16[1024,1024]{1,0:T(8,128)(2,1)} async-done(((bf16[256,1024]{1,0:T(8,128)(2,1)}), bf16[1024,1024]{1,0:T(8,128)(2,1)}) %all-gather.32.cloned.1.call-update) | async-done | bytes 2097168 | tf_op jit(solution)/shard_map/all_gather | solution.py:277
  704.7 2.4 convolution_convert_fusion.4
  707.2 8.1 multiply_reduce_fusion.1
  715.3 4.5 multiply_convert_fusion.1
  723.9 2.5 fusion.8
  726.4 4.3 multiply_reduce_fusion
  730.7 2.4 convolution_convert_fusion.5
  733.2 7.7 multiply_reduce_fusion.3
  740.9 4.5 multiply_convert_fusion.3
  751.2 4.4 multiply_reduce_fusion.2
  762.9 6.9 multiply_convert_fusion
  802.2 4.8 fusion.165
  807.1 4.5 convolution_add_fusion.2
  813.2 4.8 fusion.118
  818.1 4.4 convolution_add_fusion.1
  824.1 4.2 fusion.166
  828.3 4.6 convolution_add_fusion
  836.4 2.9 convolution_add_fusion.5
  841.5 39.9 %all-reduce.16 = (f32[1024]{0:T(1024)S(1)}, f32[1024]{0:T(1024)S(1)}, f32[1024]{0:T(1024)S(1)}, f32[4096]{0:T(1024)S(1)}, f32[4096]{0:T(1024)S(1)}) all-reduce(f32[1024]{0:T(1024)S(1)} %add_dynamic-update-slice_fusion.2, f32[1024]{0:T(1024)S(1)} %add.462, ...), channel_id=19, replica_groups=mesh['dp'=8,'tensor'=4] {'dp','tensor'}, use_global_device_ids=true, to_apply=%region_67.68.clone | all-reduce | flops 11264 | bytes 90112
  886.1 9.5 reduce-scatter.32.cloned.1.call-done
  897.2 65.4 %reduce-scatter.34.cloned.1.call-done = f32[128,256]{0,1:T(8,128)} async-done(((f32[1024,256]{0,1:T(8,128)}), f32[128,256]{0,1:T(8,128)}) %reduce-scatter.34.cloned.1.call-update) | async-done | bytes 131088 | tf_op jit(solution)/shard_map/reduce_scatter | solution.py:343
  964.2 31.1 %reduce-scatter.26.cloned.1.call-done = bf16[256,1024]{1,0:T(8,128)(2,1)} async-done(((bf16[1024,1024]{1,0:T(8,128)(2,1)}), bf16[256,1024]{1,0:T(8,128)(2,1)}) %reduce-scatter.26.cloned.1.call-update) | async-done | bytes 524304 | tf_op jit(solution)/shard_map/reduce_scatter | solution.py:16
  995.4 33.5 %reduce-scatter.30.cloned.1.call-done = bf16[256,1024]{1,0:T(8,128)(2,1)} async-done(((bf16[1024,1024]{1,0:T(8,128)(2,1)}), bf16[256,1024]{1,0:T(8,128)(2,1)}) %reduce-scatter.30.cloned.1.call-update) | async-done | bytes 524304 | tf_op jit(solution)/shard_map/reduce_scatter | solution.py:16
  1031.6 89.8 %reduce-scatter.40.cloned.1.call-done = f32[128,1024]{1,0:T(8,128)} async-done(((f32[1024,1024]{1,0:T(8,128)}), f32[128,1024]{1,0:T(8,128)}) %reduce-scatter.40.cloned.1.call-update) | async-done | bytes 524304 | tf_op jit(solution)/shard_map/reduce_scatter | solution.py:346
  1121.4 92.1 %reduce-scatter.42.cloned.1.call-done = f32[128,1024]{1,0:T(8,128)} async-done(((f32[1024,1024]{1,0:T(8,128)}), f32[128,1024]{1,0:T(8,128)}) %reduce-scatter.42.cloned.1.call-update) | async-done | bytes 524304 | tf_op jit(solution)/shard_map/reduce_scatter | solution.py:347
  1213.5 92.5 %reduce-scatter.44.cloned.1.call-done = f32[1024,128]{1,0:T(8,128)} async-done(((f32[1024,1024]{1,0:T(8,128)}), f32[1024,128]{1,0:T(8,128)}) %reduce-scatter.44.cloned.1.call-update) | async-done | bytes 524304 | tf_op jit(solution)/shard_map/reduce_scatter | solution.py:348
  1306.0 68.3 %reduce-scatter.38.cloned.1.call-done = f32[256,128]{1,0:T(8,128)} async-done(((f32[256,1024]{1,0:T(8,128)}), f32[256,128]{1,0:T(8,128)}) %reduce-scatter.38.cloned.1.call-update) | async-done | bytes 131088 | tf_op jit(solution)/shard_map/reduce_scatter | solution.py:345
  (554 shorter events, 153.7 us)
Async XLA Ops:
  8.0 115.7 %copy-start.114 = (bf16[128,256]{1,0:T(8,128)(2,1)S(1)}, bf16[128,256]{1,0:T(8,128)(2,1)}, u32[]{:S(2)}) copy-start(bf16[128,256]{1,0:T(8,128)(2,1)} %param.20) | copy-start | bytes 196612
  8.0 149.4 %copy-start.115 = (bf16[256,128]{1,0:T(8,128)(2,1)S(1)}, bf16[256,128]{1,0:T(8,128)(2,1)}, u32[]{:S(2)}) copy-start(bf16[256,128]{1,0:T(8,128)(2,1)} %param.21) | copy-start | bytes 196612
  8.0 181.2 %all-gather.34.cloned.1.call-start = ((), (), s32[]{:S(2)}) async-start(), calls=%async_computation.39 | async-start | bytes 2621440 | tf_op jit(solution)/shard_map/all_gather | solution.py:197
  10.3 185.3 %all-gather.36.cloned.1.call-start = ((), (), s32[]{:S(2)}) async-start(), calls=%async_computation.40 | async-start | bytes 2621440 | tf_op jit(solution)/shard_map/all_gather | solution.py:197
  11.1 239.2 %reduce-scatter.16.cloned.1.call-start = ((), (), s32[]{:S(2)}) async-start(), calls=%async_computation.15 | async-start | bytes 2621440 | tf_op jit(solution)/shard_map/reduce_scatter | solution.py:16
  59.5 143.6 %copy-start.112 = (f32[4,64]{1,0:T(4,128)}, f32[4,64]{1,0:T(4,128)S(1)}, u32[]{:S(2)}) copy-start(f32[4,64]{1,0:T(4,128)S(1)} %mul.1299) | copy-start | bytes 3076
  92.0 103.6 %copy-start.17 = (bf16[1024,256]{1,0:T(8,128)(2,1)}, bf16[1024,256]{1,0:T(8,128)(2,1)S(1)}, u32[]{:S(2)}) copy-start(bf16[1024,256]{1,0:T(8,128)(2,1)S(1)} %all_gather.64) | copy-start | bytes 1572868
  123.7 74.6 %copy-start.15 = (bf16[1024,256]{1,0:T(8,128)(2,1)}, bf16[1024,256]{1,0:T(8,128)(2,1)S(1)}, u32[]{:S(2)}) copy-start(bf16[1024,256]{1,0:T(8,128)(2,1)S(1)} %all_gather.65) | copy-start | bytes 1572868
  187.5 13.3 copy-start.84
  187.5 13.3 copy-start.86
  195.3 7.9 copy-start.23
  195.3 7.8 copy-start.25
  195.6 7.6 copy-start.96
  203.5 202.2 %copy-start.21 = (bf16[1024,4,64]{0,2,1:T(8,128)(2,1)}, bf16[1024,4,64]{0,2,1:T(8,128)(2,1)S(1)}, u32[]{:S(2)}) copy-start(bf16[1024,4,64]{0,2,1:T(8,128)(2,1)S(1)} %get-tuple-element.268) | copy-start | bytes 1572868
  207.2 8.7 copy-start.1
  218.0 37.3 %copy-start.93 = (bf16[4,64,512]{2,1,0:T(8,128)(2,1)}, bf16[4,64,512]{2,1,0:T(8,128)(2,1)S(1)}, u32[]{:S(2)}) copy-start(bf16[4,64,512]{2,1,0:T(8,128)(2,1)S(1)} %fusion.93) | copy-start | bytes 786436
  218.0 33.4 %copy-start.8 = (bf16[2,256,1024]{2,1,0:T(8,128)(2,1)S(1)}, bf16[2,256,1024]{2,1,0:T(8,128)(2,1)}, u32[]{:S(2)}) copy-start(bf16[2,256,1024]{2,1,0:T(8,128)(2,1)} %param.15) | copy-start | bytes 3145732
  218.1 38.6 %copy-start.123 = (f32[128]{0:T(128)S(1)}, f32[128]{0:T(128)}, u32[]{:S(2)}) copy-start(f32[128]{0:T(128)} %param.28) | copy-start | bytes 1540
  218.1 79.4 %copy-start.124 = (f32[128]{0:T(128)S(1)}, f32[128]{0:T(128)}, u32[]{:S(2)}) copy-start(f32[128]{0:T(128)} %param.29) | copy-start | bytes 1540
  220.2 114.3 %all-gather.20.cloned.1.call-start = ((), (), s32[]{:S(2)}) async-start(), calls=%async_computation.18 | async-start | bytes 2359296 | tf_op jit(solution)/shard_map/all_gather | solution.py:152
  220.8 113.7 %all-gather.16.cloned.1.call-start = ((), (), s32[]{:S(2)}) async-start(), calls=%async_computation.16 | async-start | bytes 2621440 | tf_op jit(solution)/shard_map/all_gather | solution.py:230
  255.3 89.5 %all-gather.18.cloned.1.call-start = ((), (), s32[]{:S(2)}) async-start(), calls=%async_computation.17 | async-start | bytes 2359296 | tf_op jit(solution)/shard_map/all_gather | solution.py:151
  255.9 140.0 %all-gather.22.cloned.1.call-start = ((), (), s32[]{:S(2)}) async-start(), calls=%async_computation.19 | async-start | bytes 2359296 | tf_op jit(solution)/shard_map/all_gather | solution.py:153
  256.6 174.8 %reduce-scatter.18.cloned.1.call-start = ((), (), s32[]{:S(2)}) async-start(), calls=%async_computation.20 | async-start | bytes 2621440 | tf_op jit(solution)/shard_map/reduce_scatter | solution.py:16
  395.9 8.0 copy-start.47
  401.9 60.3 %all-gather.26.cloned.1.call-start = ((), (), s32[]{:S(2)}) async-start(), calls=%async_computation.24 | async-start | bytes 2621440 | tf_op jit(solution)/shard_map/all_gather | solution.py:251
  431.4 7.1 copy-start.39
  439.7 48.7 %reduce-scatter.20.cloned.1.call-start = ((), (), s32[]{:S(2)}) async-start(), calls=%async_computation.21 | async-start | bytes 2621440 | tf_op jit(solution)/shard_map/reduce_scatter | solution.py:16
  441.5 10.2 copy-start.74
  441.5 10.2 slice-start.8
  456.8 65.2 %reduce-scatter.24.cloned.1.call-start = ((), (), s32[]{:S(2)}) async-start(), calls=%async_computation.25 | async-start | bytes 2621440 | tf_op jit(solution)/shard_map/reduce_scatter | solution.py:16
  462.2 10.5 copy-start.133
  479.7 69.7 %all-gather.24.cloned.1.call-start = ((), (), s32[]{:S(2)}) async-start(), calls=%async_computation.22 | async-start | bytes 2621440 | tf_op jit(solution)/shard_map/all_gather | solution.py:230
  526.8 68.5 %reduce-scatter.22.cloned.1.call-start = ((), (), s32[]{:S(2)}) async-start(), calls=%async_computation.23 | async-start | bytes 2621440 | tf_op jit(solution)/shard_map/reduce_scatter | solution.py:16
  564.0 62.1 %all-gather.30.cloned.1.call-start = ((), (), s32[]{:S(2)}) async-start(), calls=%async_computation.28 | async-start | bytes 2621440 | tf_op jit(solution)/shard_map/all_gather | solution.py:251
  603.4 70.7 %reduce-scatter.28.cloned.1.call-start = ((), (), s32[]{:S(2)}) async-start(), calls=%async_computation.29 | async-start | bytes 2621440 | tf_op jit(solution)/shard_map/reduce_scatter | solution.py:16
  626.1 9.8 copy-start.135
  642.8 61.9 %all-gather.32.cloned.1.call-start = ((), (), s32[]{:S(2)}) async-start(), calls=%async_computation.30 | async-start | bytes 2621440 | tf_op jit(solution)/shard_map/all_gather | solution.py:277
  682.0 25.2 %copy-start.75 = (bf16[1024,256]{0,1:T(8,128)(2,1)S(1)}, bf16[1024,256]{0,1:T(8,128)(2,1)}, u32[]{:S(2)}) copy-start(bf16[1024,256]{0,1:T(8,128)(2,1)} %copy-done.74) | copy-start | bytes 1572868
  682.0 48.7 %all-gather.28.cloned.1.call-start = ((), (), s32[]{:S(2)}) async-start(), calls=%async_computation.26 | async-start | bytes 2621440 | tf_op jit(solution)/shard_map/all_gather | solution.py:277
  682.7 201.7 %reduce-scatter.36.cloned.1.call-start = ((), (), s32[]{:S(2)}) async-start(), calls=%async_computation.34 | async-start | bytes 1179648 | tf_op jit(solution)/shard_map/reduce_scatter | solution.py:344
  707.2 8.1 slice-start.10
  707.2 8.1 slice-start.11
  715.3 8.6 slice-start.6
  715.3 8.6 slice-start.7
  733.2 7.7 slice-start.4
  733.2 7.7 slice-start.5
  740.9 8.6 slice-start
  740.9 8.6 slice-start.1
  749.5 8.0 slice-start.12
  762.8 132.7 %reduce-scatter.32.cloned.1.call-start = ((), (), s32[]{:S(2)}) async-start(), calls=%async_computation.32 | async-start | bytes 1179648 | tf_op jit(solution)/shard_map/reduce_scatter | solution.py:342
  762.9 10.0 slice-start.2
  762.9 10.0 slice-start.14
  762.9 10.1 slice-start.3
  762.9 11.2 slice-start.15
  788.3 174.3 %reduce-scatter.34.cloned.1.call-start = ((), (), s32[]{:S(2)}) async-start(), calls=%async_computation.33 | async-start | bytes 1179648 | tf_op jit(solution)/shard_map/reduce_scatter | solution.py:343
  794.2 201.2 %reduce-scatter.26.cloned.1.call-start = ((), (), s32[]{:S(2)}) async-start(), calls=%async_computation.27 | async-start | bytes 2621440 | tf_op jit(solution)/shard_map/reduce_scatter | solution.py:16
  798.3 230.6 %reduce-scatter.30.cloned.1.call-start = ((), (), s32[]{:S(2)}) async-start(), calls=%async_computation.31 | async-start | bytes 2621440 | tf_op jit(solution)/shard_map/reduce_scatter | solution.py:16
  802.2 319.2 %reduce-scatter.40.cloned.1.call-start = ((), (), s32[]{:S(2)}) async-start(), calls=%async_computation.36 | async-start | bytes 4718592 | tf_op jit(solution)/shard_map/reduce_scatter | solution.py:346
  811.7 401.8 %reduce-scatter.42.cloned.1.call-start = ((), (), s32[]{:S(2)}) async-start(), calls=%async_computation.37 | async-start | bytes 4718592 | tf_op jit(solution)/shard_map/reduce_scatter | solution.py:347
  822.5 483.5 %reduce-scatter.44.cloned.1.call-start = ((), (), s32[]{:S(2)}) async-start(), calls=%async_computation.38 | async-start | bytes 4718592 | tf_op jit(solution)/shard_map/reduce_scatter | solution.py:348
  833.0 541.3 %reduce-scatter.38.cloned.1.call-start = ((), (), s32[]{:S(2)}) async-start(), calls=%async_computation.35 | async-start | bytes 1179648 | tf_op jit(solution)/shard_map/reduce_scatter | solution.py:345
  836.4 192.5 %copy-start.42 = (f32[256,1024]{1,0:T(8,128)S(1)}, f32[256,1024]{1,0:T(8,128)}, u32[]{:S(2)}) copy-start(f32[256,1024]{1,0:T(8,128)} %copy-done.41) | copy-start | bytes 3145732
  836.4 192.5 %copy-start.44 = (f32[256,1024]{1,0:T(8,128)S(1)}, f32[256,1024]{1,0:T(8,128)}, u32[]{:S(2)}) copy-start(f32[256,1024]{1,0:T(8,128)} %copy-done.43) | copy-start | bytes 3145732
  (124 other events, 384.6 us)
Sparse Core Ops, SparseCore 0:
  11.0 25.9 all-gather.33
  39.1 22.9 all-gather.35
  220.3 29.8 reduce-scatter.15
  402.0 29.3 reduce-scatter.17
  456.9 31.3 reduce-scatter.19
  490.7 31.1 reduce-scatter.23
  603.5 22.5 all-gather.29
  682.1 22.5 all-gather.31
  706.8 22.5 all-gather.27
Sparse Core Ops, SparseCore 1:
  222.8 47.7 all-gather.19
  272.6 21.0 all-gather.15
  295.7 49.1 all-gather.17
  346.9 49.0 all-gather.21
  439.7 22.4 all-gather.25
  526.9 22.4 all-gather.23
  564.1 31.2 reduce-scatter.21
  642.9 31.2 reduce-scatter.27
  762.9 64.8 reduce-scatter.35
  831.8 63.7 reduce-scatter.31
  898.8 63.7 reduce-scatter.33
  965.1 30.2 reduce-scatter.25
  997.8 31.1 reduce-scatter.29
  1033.1 88.2 reduce-scatter.39
  1125.6 87.8 reduce-scatter.41
  1217.7 88.2 reduce-scatter.43
  1310.0 64.2 reduce-scatter.37
where the time goes:
time: 1390 us; the launch traced here: 1380 us
  waiting for transfers between devices  754 us (54%)
  blocking collectives  286 us (21%)
  matrix products  203 us (15%)
  other arithmetic  82.1 us (6%)
  local copies, waits for them, and re-layouts  35.6 us (3%)
  between operations  18.2 us (1%)
    reduce_scatter x8, waiting for transfers between devices, scattered(): lax.psum_scatter(sent, axis, scatter_dimension=0, tiled=True)  215 us
    reduce_scatter x1, waiting for transfers between devices, shards(): lax.psum_scatter(totals[6], 'dp', scatter_dimension=1, tiled=True)  92.5 us
    reduce_scatter x1, waiting for transfers between devices, shards(): lax.psum_scatter(totals[5], 'dp', scatter_dimension=0, tiled=True)  92.1 us
    reduce_scatter x1, waiting for transfers between devices, shards(): lax.psum_scatter(totals[4], 'dp', scatter_dimension=0, tiled=True)  89.8 us
    unnamed x2, blocking collectives  83.2 us
    reduce_scatter x1, waiting for transfers between devices, shards(): lax.psum_scatter(totals[3], 'dp', scatter_dimension=1, tiled=True)  68.3 us
    reduce_scatter x1, waiting for transfers between devices, shards(): lax.psum_scatter(totals[1], 'dp', scatter_dimension=0, tiled=True)  65.4 us
    all_gather x1, waiting for transfers between devices, shards(): lax.all_gather(w_down, 'dp', axis=1, tiled=True)  42.3 us
  transfers between devices with their start and end apart: 26, of which 20 were waited for; matrix products, arithmetic and copies ran while one was open for 13% of the time, Pallas kernels for 0%

commit v1 on v0

v1 whole, which is shorter than its diff:
```python
import functools
import math

import jax
import jax.numpy as jnp
from jax import lax
from jax.experimental import pallas as pl
from jax.experimental.pallas import tpu as pltpu
from jax.sharding import PartitionSpec as P

DH = 64
BLOCK = 256
DOCS = 3
DOC_MAX = 512
F32 = jnp.float32
BF16 = jnp.bfloat16
MESH = pl.DeviceIdType.MESH
VMEM_LIMIT = 67043328
LOG2E = 1.4426950408889634
QB = 128
CODE = 8


def doc_places(docs):
    labels = jnp.arange(DOCS, dtype=jnp.int32)
    member = (docs[..., :, None] == labels).astype(jnp.int32)
    counts = jnp.sum(member, axis=-2)
    starts = jnp.cumsum(counts, axis=-1) - counts
    first = jnp.sum(member * starts[..., None, :], axis=-1)
    return jnp.arange(docs.shape[-1], dtype=jnp.int32) - first


def nn(a, b):
    return jnp.dot(a, b, preferred_element_type=F32)


def nt(a, b):
    return lax.dot_general(a, b, (((1,), (1,)), ((), ())), preferred_element_type=F32)


def tn(a, b):
    return lax.dot_general(a, b, (((0,), (0,)), ((), ())), preferred_element_type=F32)


def split_sum(vals, ones):
    high = vals.astype(BF16)
    low = (vals - high.astype(F32)).astype(BF16)
    return nn(high, ones) + nn(low, ones)


def lane_iota(shape):
    return lax.broadcasted_iota(jnp.int32, shape, len(shape) - 1)


def head_ones():
    rows = lax.broadcasted_iota(jnp.int32, (128, 128), 0) // DH
    cols = lax.broadcasted_iota(jnp.int32, (128, 128), 1) // DH
    return jnp.where(rows == cols, 1.0, 0.0).astype(BF16)


def partner(vals):
    low = lane_iota(vals.shape) % DH < DH // 2
    return jnp.where(low, pltpu.roll(vals, 128 - DH // 2, 1), pltpu.roll(vals, DH // 2, 1))


def turns(table):
    lane = lane_iota(table.shape)
    both = jnp.where(lane < DH, table, pltpu.roll(table, DH, 1))
    low = lane % DH < DH // 2
    cosine = jnp.where(low, both, pltpu.roll(both, DH // 2, 1))
    sine = jnp.where(low, -pltpu.roll(both, 128 - DH // 2, 1), both)
    return cosine, sine


class Place:
    def __init__(self, n):
        self.n = n
        self.t = lax.axis_index("tensor")
        self.d = lax.axis_index("dp")
        t, d = self.t, self.d
        self.sib = t + 1 - 2 * (t % 2)
        self.yp = (t + 2) % 4
        self.diag = (self.sib + 2) % 4
        self.xi = d % 2
        self.z = d // 2
        self.nz = n // 2
        self.xn = d + 1 - 2 * (d % 2)
        self.zpeers = [2 * ((self.z + k) % self.nz) + self.xi for k in range(1, self.nz)]
        self.dpeers = [(d + k) % n for k in range(1, n)]
        self.tpeers = [(t + k) % 4 for k in range(1, 4)]

    def barrier(self):
        sem = pltpu.get_barrier_semaphore()
        for peer in self.dpeers:
            pl.semaphore_signal(sem, inc=1, device_id={"dp": peer}, device_id_type=MESH)
        for peer in self.tpeers:
            pl.semaphore_signal(sem, inc=1, device_id={"tensor": peer}, device_id_type=MESH)
        pl.semaphore_wait(sem, self.n + 2)


def remote(src, dst, ssem, rsem, **where):
    return pltpu.make_async_remote_copy(
        src_ref=src, dst_ref=dst, send_sem=ssem, recv_sem=rsem, device_id=where, device_id_type=MESH
    )


class Gather:
    def __init__(self, place, whole, ssem, rsem, rows):
        self.p, self.whole, self.ssem, self.rsem, self.rows = place, whole, ssem, rsem, rows

    def at(self, index):
        return self.whole.at[pl.ds(pl.multiple_of(index * self.rows, self.rows), self.rows)]

    def start(self, own):
        p = self.p
        self.c_yp = remote(own, self.at(p.t), self.ssem.at[1], self.rsem.at[1], tensor=p.yp)
        self.c_sib = remote(own, self.at(p.t), self.ssem.at[0], self.rsem.at[0], tensor=p.sib)
        self.c_yp.start()
        self.c_sib.start()

    def wait(self, step):
        p = self.p
        if step == 1:
            remote(self.at(p.sib), self.at(p.sib), self.ssem.at[0], self.rsem.at[0], tensor=p.sib).wait_recv()
        if step == 2:
            remote(self.at(p.yp), self.at(p.yp), self.ssem.at[1], self.rsem.at[1], tensor=p.yp).wait_recv()
            self.c_fwd = remote(
                self.at(p.yp), self.at(p.yp), self.ssem.at[2], self.rsem.at[2], tensor=p.sib
            )
            self.c_fwd.start()
        if step == 3:
            remote(self.at(p.diag), self.at(p.diag), self.ssem.at[2], self.rsem.at[2], tensor=p.sib).wait_recv()

    def drain(self):
        self.c_yp.wait_send()
        self.c_sib.wait_send()
        self.c_fwd.wait_send()

    def order(self):
        p = self.p
        return (p.t, p.sib, p.yp, p.diag)


class Scatter:
    def __init__(self, place, sbuf, rbuf, ssem, rsem):
        self.p, self.sbuf, self.rbuf, self.ssem, self.rsem = place, sbuf, rbuf, ssem, rsem
        self.copies = []

    def send(self, slot, **where):
        copy = remote(
            self.sbuf.at[slot], self.rbuf.at[slot], self.ssem.at[slot], self.rsem.at[slot], **where
        )
        copy.start()
        self.copies.append(copy)

    def arrive(self, slot):
        remote(
            self.rbuf.at[slot], self.rbuf.at[slot], self.ssem.at[slot], self.rsem.at[slot],
            tensor=self.p.sib,
        ).wait_recv()

    def run(self, part, own):
        p = self.p
        self.sbuf[0] = part(p.diag).astype(BF16)
        self.send(0, tensor=p.sib)
        self.sbuf[1] = part(p.sib).astype(BF16)
        self.send(1, tensor=p.sib)
        across = part(p.yp)
        self.arrive(0)
        self.sbuf[2] = (across + self.rbuf[0].astype(F32)).astype(BF16)
        self.send(2, tensor=p.yp)
        mine = part(p.t)
        self.arrive(1)
        own[...] = mine + self.rbuf[1].astype(F32)

    def finish(self):
        self.arrive(2)
        for copy in self.copies:
            copy.wait_send()


def rows_of(ref, index, rows):
    return ref[pl.ds(pl.multiple_of(index * rows, rows), rows)]


def mean_sq(vals):
    return jnp.mean(vals * vals, axis=-1, keepdims=True)


def fold8(vals):
    total = vals[0:8]
    for k in range(1, vals.shape[0] // 8):
        total = total + vals[8 * k : 8 * k + 8]
    return total


def fwd_kernel(
    n,
    wsh, hid, og, small, table, irow,
    o_out, o_w, o_x, o_q, o_k, o_v, o_rq, o_rk, o_lrow, o_mixed, o_mid, o_up, o_gate, o_inner,
    o_attn, o_gmd, o_gm, o_gm0, o_vec, o_acc,
    w, x, q, k, v, rq, rk, lcol, mixed, mid, up, gate, inner,
    attn, midf, mlp, gmd, gm, gm0, vec, acc, sall, tab, ogv, outv, ir, qm, sbuf, rbuf,
    wsend, wrecv, wloc, small_s, small_r, lsem, agx_s, agx_r, agm_s, agm_r, agg_s, agg_r,
    rsa_s, rsa_r, rsm_s, rsm_r, osem,
):
    p = Place(n)
    nz = p.nz
    mbs, rows, width = hid.shape
    seq = x.shape[1]
    hw = q.shape[2]
    shard = wsh.shape[1]
    heads = hw // DH
    groups = wsh.shape[0]
    hidden = up.shape[2]

    def wat(g, index):
        return w.at[g, pl.ds(pl.multiple_of(index * shard, shard), shard)]

    local = []

    def lcopy(src, dst):
        copy = pltpu.make_async_copy(src, dst, lsem.at[len(local)])
        copy.start()
        local.append(copy)
        return copy

    outs = []

    def ocopy(src, dst):
        copy = pltpu.make_async_copy(src, dst, osem.at[len(outs)])
        copy.start()
        outs.append(copy)

    p.barrier()

    gx = [Gather(p, x.at[m], agx_s.at[m], agx_r.at[m], rows) for m in range(mbs)]
    gmi = [Gather(p, mid.at[m], agm_s.at[m], agm_r.at[m], rows) for m in range(mbs)]
    flat = 4 * p.d + p.t
    small_own = lcopy(small, sall.at[flat])
    small_t = [
        remote(small, sall.at[flat], small_s.at[i], small_r.at[i], tensor=peer)
        for i, peer in enumerate(p.tpeers)
    ]
    for copy in small_t:
        copy.start()
    gx[0].start(hid.at[0])
    sends = []

    def wsend_to(g, i, src, index, peer):
        copy = remote(src, wat(g, index), wsend.at[g, i], wrecv.at[g, index], dp=peer)
        copy.start()
        sends.append(copy)

    def relay(g):
        for i, peer in enumerate(p.zpeers):
            remote(wat(g, peer), wat(g, peer), wsend.at[g, 0], wrecv.at[g, peer], dp=p.xn).wait_recv()
            wsend_to(g, nz + i, wat(g, peer), peer, p.xn)

    wown = []
    for g in range(groups):
        for i, peer in enumerate(p.zpeers):
            wsend_to(g, i, wsh.at[g], p.d, peer)
        if g == 0:
            wsend_to(0, nz - 1, wsh.at[0], p.d, p.xn)
            gx[1].start(hid.at[1])
    for g in range(groups):
        copy = pltpu.make_async_copy(wsh.at[g], wat(g, p.d), wloc.at[g])
        copy.start()
        wown.append(copy)
    xown = [lcopy(hid.at[m], gx[m].at(p.t)) for m in range(mbs)]
    tables = [lcopy(table, tab), lcopy(irow, ir)]
    og_in = lcopy(og, ogv)
    for i, peer in enumerate(p.tpeers):
        src = (p.t + 4 - (i + 1)) % 4
        remote(sall.at[4 * p.d + src], sall.at[4 * p.d + src], small_s.at[i], small_r.at[i], tensor=peer).wait_recv()
    small_own.wait()
    small_d = []
    for i, peer in enumerate(p.dpeers):
        part = sall.at[pl.ds(4 * p.d, 4)]
        copy = remote(part, part, small_s.at[3 + i], small_r.at[3 + i], dp=peer)
        copy.start()
        small_d.append(copy)

    def wready(g):
        remote(wat(g, p.xn), wat(g, p.xn), wsend.at[g, 0], wrecv.at[g, p.xn], dp=p.xn).wait_recv()
        for peer in p.zpeers:
            other = peer + 1 - 2 * p.xi
            remote(wat(g, other), wat(g, other), wsend.at[g, 0], wrecv.at[g, other], dp=p.xn).wait_recv()
        wown[g].wait()
        ocopy(w.at[g], o_w.at[g])

    relay(0)
    for i, peer in enumerate(p.dpeers):
        src = (p.d + n - (i + 1)) % n
        part = sall.at[pl.ds(4 * src, 4)]
        remote(part, part, small_s.at[3 + i], small_r.at[3 + i], dp=peer).wait_recv()
    every = 4 * n

    def gathered(row, base, count, lanes):
        per = count // (lanes // 128)
        for r in range(lanes // 128):
            total = sall[base + r * per, row : row + 1, :]
            for j in range(1, per):
                total = total + sall[base + r * per + j, row : row + 1, :]
            vec[row : row + 1, 128 * r : 128 * r + 128] = total

    gathered(0, p.t * n, n, hw)
    gathered(1, 0, every, width)
    gathered(2, 0, every, width)
    gathered(3, p.t * n, n, hidden)
    gathered(4, p.t * n, n, hidden)
    acc[...] = jnp.zeros_like(acc)
    for copy in tables:
        copy.wait()
    wready(0)
    wsend_to(1, nz - 1, wsh.at[1], p.d, p.xn)

    ones = head_ones()

    def stage_qkv(m):
        for step, index in enumerate(gx[m].order()):
            gx[m].wait(step)
            if step == 0:
                xown[m].wait()
            at = pl.ds(pl.multiple_of(index * rows, rows), rows)
            xb = x[m, at, :]
            cb, sb = turns(tab[m, at, :])
            for which, (dst, rdst) in enumerate(((q, rq), (k, rk))):
                raw = nn(xb, w[0, :, which * hw : (which + 1) * hw])
                for half in range(hw // 128):
                    lanes = slice(128 * half, 128 * half + 128)
                    piece = raw[:, lanes]
                    turned = piece * cb + partner(piece) * sb
                    scale = lax.rsqrt(split_sum(turned * turned, ones) + 1e-06)
                    rdst[m, at, lanes] = scale.astype(BF16)
                    dst[m, at, lanes] = (turned * scale * vec[0:1, lanes]).astype(BF16)
            v[m, at, :] = nn(xb, w[0, :, 2 * hw : 3 * hw]).astype(BF16)

    win = seq - 128
    c_exp = math.sqrt(DH) * LOG2E

    def attend(m):
        def body(b, carry):
            at = pl.ds(pl.multiple_of(b * QB, QB), QB)
            keys = pl.ds(pl.multiple_of(((b + 3) // 8) * 128, 128), win)
            ccol = tab[m, at, DH : DH + 1]
            lcol_ = tab[m, at, DH + 1 : DH + 2]
            crow = ir[m, 0:1, keys]
            bias = jnp.where((crow <= ccol) & (crow >= lcol_), 0.0, -1e30)
            qb = q[m, at, :]
            lane = lane_iota((QB, hw)) // DH
            for h in range(heads):
                qm[h * QB : (h + 1) * QB, :] = jnp.where(lane == h, qb, jnp.zeros_like(qb))
            kb = k[m, keys, :]
            vb = v[m, keys, :]
            total = jnp.zeros((QB, hw), F32)
            lsum = jnp.zeros((QB, 128), F32)
            lane_l = lane_iota((QB, 128))
            for h in range(heads):
                scores = nt(qm[h * QB : (h + 1) * QB, :], kb)
                expo = jnp.exp2(scores * c_exp + bias)
                inv = 1.0 / jnp.sum(expo, axis=-1, keepdims=True)
                part = nn(expo.astype(BF16), vb)
                total = jnp.where(lane == h, part * inv, total)
                lsum = jnp.where(lane_l == h, inv, lsum)
            mixed[m, at, :] = total.astype(BF16)
            lcol[m, at, :] = lsum
            return carry

        lax.fori_loop(0, seq // QB, body, 0)

    sc_a = [Scatter(p, sbuf.at[m], rbuf.at[m], rsa_s.at[m], rsa_r.at[m]) for m in range(mbs)]
    sc_m = [Scatter(p, sbuf.at[m], rbuf.at[m], rsm_s.at[m], rsm_r.at[m]) for m in range(mbs)]

    def stage_o(m):
        sc_a[m].run(
            lambda index: nt(rows_of(mixed.at[m], index, rows), w[0, :, 3 * hw : 3 * hw + hw]),
            attn.at[m],
        )

    chunk = 32

    def stage_mid(m):
        sc_a[m].finish()
        base = p.t * rows

        def body(i, carry):
            at = pl.ds(pl.multiple_of(i * chunk, chunk), chunk)
            own = pl.ds(pl.multiple_of(base + i * chunk, chunk), chunk)
            a = attn[m, at, :] + rbuf[m, 2, at, :].astype(F32)
            attn[m, at, :] = a
            h = x[m, own, :].astype(F32)
            na = a * lax.rsqrt(mean_sq(a) + 1e-06)
            zz = h + vec[1:2, :] * (na - h)
            out = zz * lax.rsqrt(mean_sq(zz) + 1e-06)
            midf[m, at, :] = out
            mid[m, own, :] = out.astype(BF16)
            return carry

        lax.fori_loop(0, rows // chunk, body, 0)
        gmi[m].start(gmi[m].at(p.t))

    cols = 256

    def stage_up(m):
        for step, index in enumerate(gmi[m].order()):
            gmi[m].wait(step)
            at = pl.ds(pl.multiple_of(index * rows, rows), rows)

            def body(c, carry):
                lanes = pl.ds(pl.multiple_of(c * cols, cols), cols)
                mb = mid[m, at, :]
                u = nn(mb, w[1, :, lanes])
                g = nn(mb, w[2, :, lanes])
                up[m, at, lanes] = u.astype(BF16)
                gate[m, at, lanes] = g.astype(BF16)
                gs = g * vec[4:5, lanes]
                inner[m, at, lanes] = ((u * vec[3:4, lanes]) * (gs / (1.0 + jnp.exp(-gs)))).astype(BF16)
                return carry

            lax.fori_loop(0, hidden // cols, body, 0)

    def stage_down(m):
        sc_m[m].run(lambda index: nt(rows_of(inner.at[m], index, rows), w[3]), mlp.at[m])

    gg = Gather(p, gm0, agg_s, agg_r, rows)

    def stage_end(m):
        sc_m[m].finish()

        def body(i, carry):
            at = pl.ds(pl.multiple_of(i * chunk, chunk), chunk)
            a = mlp[m, at, :] + rbuf[m, 2, at, :].astype(F32)
            h = midf[m, at, :]
            ra = lax.rsqrt(mean_sq(a) + 1e-06)
            na = a * ra
            al = vec[2:3, :]
            zz = h + al * (na - h)
            rz = lax.rsqrt(mean_sq(zz) + 1e-06)
            out = zz * rz
            outv[m, at, :] = out.astype(BF16)
            cot = ogv[m, at, :].astype(F32)
            dz = rz * (cot - out * jnp.mean(cot * out, axis=-1, keepdims=True))
            dn = al * dz
            acc[0:8, :] += fold8(dz * (na - h))
            gmd[m, at, :] = dz - dn
            grad = (ra * (dn - na * jnp.mean(dn * na, axis=-1, keepdims=True))).astype(BF16)
            gm[m, at, :] = grad
            if m == 0:
                gm0[pl.ds(pl.multiple_of(p.t * rows + i * chunk, chunk), chunk), :] = grad
            return carry

        lax.fori_loop(0, rows // chunk, body, 0)
        if m == 0:
            gg.start(gg.at(p.t))

    stage_qkv(0)
    attend(0)
    stage_o(0)
    relay(1)
    wsend_to(2, nz - 1, wsh.at[2], p.d, p.xn)
    stage_qkv(1)
    relay(2)
    wsend_to(3, nz - 1, wsh.at[3], p.d, p.xn)
    attend(1)
    relay(3)
    stage_mid(0)
    stage_o(1)
    for m in range(mbs):
        ocopy(x.at[m], o_x.at[m])
        ocopy(q.at[m], o_q.at[m])
        ocopy(k.at[m], o_k.at[m])
        ocopy(v.at[m], o_v.at[m])
        ocopy(rq.at[m], o_rq.at[m])
        ocopy(rk.at[m], o_rk.at[m])
        ocopy(mixed.at[m], o_mixed.at[m])
    ocopy(vec, o_vec)
    wready(1)
    wready(2)
    stage_up(0)
    stage_mid(1)
    wready(3)
    stage_down(0)
    stage_up(1)
    og_in.wait()
    stage_end(0)
    ocopy(mid.at[0], o_mid.at[0])
    ocopy(up.at[0], o_up.at[0])
    ocopy(gate.at[0], o_gate.at[0])
    ocopy(inner.at[0], o_inner.at[0])
    stage_down(1)
    for m in range(mbs):
        lrow = jnp.transpose(lcol[m], (1, 0))
        lcol[m, 0:8, 0:128] = lrow[0:8, 0:128]
        for j in range(1, seq // 128):
            lcol[m, 8 * j : 8 * j + 8, 0:128] = lrow[0:8, 128 * j : 128 * j + 128]
        ocopy(lcol.at[m, pl.ds(0, seq // 16)], o_lrow.at[m])
    ocopy(mid.at[1], o_mid.at[1])
    ocopy(up.at[1], o_up.at[1])
    ocopy(gate.at[1], o_gate.at[1])
    ocopy(inner.at[1], o_inner.at[1])
    ocopy(attn, o_attn)
    for step in range(1, 3):
        gg.wait(step)
    stage_end(1)
    ocopy(outv, o_out)
    ocopy(gmd, o_gmd)
    ocopy(gm, o_gm)
    ocopy(acc, o_acc)
    gg.wait(3)
    ocopy(gm0, o_gm0)
    for gather in gx + gmi + [gg]:
        gather.drain()
    for copy in sends + small_t + small_d:
        copy.wait_send()
    for copy in outs:
        copy.wait()


def bwd_kernel(
    n,
    hid, table, irow, i_w, i_x, i_q, i_k, i_v, i_rq, i_rk, i_lrow, i_mixed, i_mid, i_up, i_gate,
    i_inner, i_attn, i_gmd, i_gm, i_gm0, i_vec, i_acc,
    o_in, o_gq, o_gk, o_gv, o_go, o_gu, o_gg, o_gd, o_tv,
    w, q, k, v, rq, rk, lrow, mixed, up, gate, inner, attn, gmd, gm, ga, vec, acc,
    tab, ir, kt, dqt, dk, dv, outv, xrecv, zrecv, vsend, vrecv, tv, sbuf, rbuf,
    lsem, agg_s, agg_r, aga_s, aga_r, rsm_s, rsm_r, rsi_s, rsi_r, xs, xr, zs, zr, vs, vr, osem,
):
    p = Place(n)
    nz = p.nz
    mbs, rows, width = hid.shape
    seq = q.shape[1]
    hw = q.shape[2]
    heads = hw // DH
    hidden = up.shape[2]
    groups = w.shape[0]
    shard = width // n
    gmix = [inner.at[m, :, pl.ds(0, hw)] for m in range(mbs)]
    pts, dss = (inner.at[m, pl.ds(0, seq - 128), pl.ds(hw, heads * QB)] for m in range(2))
    qs, gs = (
        inner.at[0, pl.ds(i * heads * QB, heads * QB), pl.ds(hw + heads * QB, hw)] for i in range(2)
    )

    local = []

    def lcopy(src, dst):
        copy = pltpu.make_async_copy(src, dst, lsem.at[len(local)])
        copy.start()
        local.append(copy)
        return copy

    outs = []

    def ocopy(src, dst):
        copy = pltpu.make_async_copy(src, dst, osem.at[len(outs)])
        copy.start()
        outs.append(copy)

    l_gm0 = lcopy(i_gm0, gm.at[0])
    l_w3 = lcopy(i_w.at[3], w.at[3])
    l_ug = [[lcopy(i_up.at[m], up.at[m]), lcopy(i_gate.at[m], gate.at[m])] for m in range(mbs)]
    l_vec = [lcopy(i_vec, vec), lcopy(i_acc, acc)]
    p.barrier()
    gg = Gather(p, gm.at[1], agg_s, agg_r, rows)
    gg.start(i_gm.at[1])
    l_gm1 = lcopy(i_gm.at[1], gg.at(p.t))
    l_w12 = [lcopy(i_w.at[1], w.at[1]), lcopy(i_w.at[2], w.at[2])]
    l_inner = [lcopy(i_inner.at[m], inner.at[m]) for m in range(mbs)]
    l_rows = [lcopy(i_attn, attn), lcopy(i_gmd, gmd)]
    l_w0 = lcopy(i_w.at[0], w.at[0])
    l_att = [
        [
            lcopy(src.at[m], dst.at[m])
            for src, dst in ((i_q, q), (i_k, k), (i_v, v), (i_rq, rq), (i_rk, rk), (i_lrow, lrow), (i_mixed, mixed))
        ]
        for m in range(mbs)
    ]
    l_tab = [lcopy(table, tab), lcopy(irow, ir)]

    gga = [Gather(p, ga.at[m], aga_s.at[m], aga_r.at[m], rows) for m in range(mbs)]
    l_hid = [lcopy(hid.at[m], gga[m].at(p.t)) for m in range(mbs)]
    sc_m = [Scatter(p, sbuf.at[m], rbuf.at[m], rsm_s.at[m], rsm_r.at[m]) for m in range(mbs)]
    sc_i = [Scatter(p, sbuf.at[m], rbuf.at[m], rsi_s.at[m], rsi_r.at[m]) for m in range(mbs)]
    cols = 256
    chunk = 32

    def stage_inner(m):
        for step, index in enumerate((p.t, p.sib, p.yp, p.diag)):
            if m == 1:
                gg.wait(step)
                if step == 0:
                    l_gm1.wait()
            at = pl.ds(pl.multiple_of(index * rows, rows), rows)

            def body(c, carry):
                lanes = pl.ds(pl.multiple_of(c * cols, cols), cols)
                gi = nn(gm[m, at, :], w[3, :, lanes])
                u = up[m, at, lanes].astype(F32)
                g = gate[m, at, lanes].astype(F32)
                su = vec[3:4, lanes]
                sg = vec[4:5, lanes]
                gsc = g * sg
                sig = 1.0 / (1.0 + jnp.exp(-gsc))
                gu = gi * (gsc * sig)
                ggs = gi * (u * su) * sig * (1.0 + gsc * (1.0 - sig))
                acc[16:24, lanes] += fold8(gu * u)
                acc[24:32, lanes] += fold8(ggs * g)
                up[m, at, lanes] = (gu * su).astype(BF16)
                gate[m, at, lanes] = (ggs * sg).astype(BF16)
                return carry

            lax.fori_loop(0, hidden // cols, body, 0)

    def stage_back(m):
        sc_m[m].run(
            lambda index: nt(rows_of(up.at[m], index, rows), w[1]) + nt(rows_of(gate.at[m], index, rows), w[2]),
            outv.at[m],
        )

    def stage_attn(m):
        sc_m[m].finish()
        base = p.t * rows

        def body(i, carry):
            at = pl.ds(pl.multiple_of(i * chunk, chunk), chunk)
            own = pl.ds(pl.multiple_of(base + i * chunk, chunk), chunk)
            cot = gmd[m, at, :] + outv[m, at, :] + rbuf[m, 2, at, :].astype(F32)
            a = attn[m, at, :]
            h = ga[m, own, :].astype(F32)
            ra = lax.rsqrt(mean_sq(a) + 1e-06)
            na = a * ra
            al = vec[1:2, :]
            zz = h + al * (na - h)
            rz = lax.rsqrt(mean_sq(zz) + 1e-06)
            out = zz * rz
            dz = rz * (cot - out * jnp.mean(cot * out, axis=-1, keepdims=True))
            dn = al * dz
            acc[8:16, :] += fold8(dz * (na - h))
            gmd[m, at, :] = dz - dn
            ga[m, own, :] = (ra * (dn - na * jnp.mean(dn * na, axis=-1, keepdims=True))).astype(BF16)
            return carry

        lax.fori_loop(0, rows // chunk, body, 0)
        gga[m].start(gga[m].at(p.t))

    def stage_mixed(m):
        for step, index in enumerate(gga[m].order()):
            gga[m].wait(step)
            at = pl.ds(pl.multiple_of(index * rows, rows), rows)
            gmix[m][at, :] = nn(ga[m, at, :], w[0, :, 3 * hw : 4 * hw]).astype(BF16)

    win = seq - 128
    c_exp = math.sqrt(DH) * LOG2E
    ones = head_ones()

    def attend(m):
        kt[...] = jnp.transpose(k[m], (1, 0))
        dk[...] = jnp.zeros_like(dk)
        dv[...] = jnp.zeros_like(dv)

        def body(b, carry):
            at = pl.ds(pl.multiple_of(b * QB, QB), QB)
            keys = pl.ds(pl.multiple_of(((b + 3) // 8) * 128, 128), win)
            crow = ir[m, 0:1, at]
            lrow_ = ir[m, 1:2, at]
            ccol = tab[m, keys, DH : DH + 1]
            bias = jnp.where((ccol <= crow) & (ccol >= lrow_), 0.0, -1e30)
            qb = q[m, at, :]
            gb = gmix[m][at, :]
            lane = lane_iota((QB, hw)) // DH
            for h in range(heads):
                qs[h * QB : (h + 1) * QB, :] = jnp.where(lane == h, qb, jnp.zeros_like(qb))
                gs[h * QB : (h + 1) * QB, :] = jnp.where(lane == h, gb, jnp.zeros_like(gb))
            kb = k[m, keys, :]
            vb = v[m, keys, :]
            for h in range(heads):
                hl = slice(h * QB, (h + 1) * QB)
                scores = nt(kb, qs[hl, :])
                inv = lrow[m, pl.ds(pl.multiple_of(b * 8, 8), 8), :][h : h + 1, :]
                pt = jnp.exp2(scores * c_exp + bias) * inv
                dpt = nt(vb, gs[hl, :])
                delta = jnp.sum(pt * dpt, axis=0, keepdims=True)
                dst = (pt * (dpt - delta)).astype(BF16)
                pts[:, hl] = pt.astype(BF16)
                dss[:, hl] = dst
                dqt[h * DH : (h + 1) * DH, at] = nn(kt[h * DH : (h + 1) * DH, keys], dst)
            dv[keys, :] += nn(pts[...], gs[...])
            dk[keys, :] += nn(dss[...], qs[...])
            return carry

        lax.fori_loop(0, seq // QB, body, 0)

        step = 256

        def after(i, carry):
            at = pl.ds(pl.multiple_of(i * step, step), step)
            cb, sb = turns(tab[m, at, :])
            v[m, at, :] = dv[at, :].astype(BF16)
            for which in range(2):
                src = (q, k)[which]
                rsc = (rq, rk)[which]
                for half in range(hw // 128):
                    lanes = slice(128 * half, 128 * half + 128)
                    if which == 0:
                        grad = jnp.transpose(dqt[lanes, at], (1, 0)) * math.sqrt(DH)
                    else:
                        grad = dk[at, lanes] * math.sqrt(DH)
                    gain = vec[0:1, lanes]
                    unit = src[m, at, lanes].astype(F32) / gain
                    acc[32:40, lanes] += fold8(grad * unit)
                    dn = grad * gain
                    dy = rsc[m, at, lanes].astype(F32) * (dn - unit * split_sum(dn * unit, ones))
                    src[m, at, lanes] = (dy * cb - partner(dy) * sb).astype(BF16)
            return carry

        lax.fori_loop(0, seq // step, after, 0)

    def stage_in(m):
        def part(index):
            at = pl.ds(pl.multiple_of(index * rows, rows), rows)
            return (
                nt(q[m, at, :], w[0, :, 0:hw])
                + nt(k[m, at, :], w[0, :, hw : 2 * hw])
                + nt(v[m, at, :], w[0, :, 2 * hw : 3 * hw])
            )

        sc_i[m].run(part, outv.at[m])

    def stage_out(m):
        sc_i[m].finish()

        def body(i, carry):
            at = pl.ds(pl.multiple_of(i * chunk, chunk), chunk)
            total = gmd[m, at, :] + outv[m, at, :] + rbuf[m, 2, at, :].astype(F32)
            sbuf[m, 0, at, :] = total.astype(BF16)
            return carry

        lax.fori_loop(0, rows // chunk, body, 0)
        ocopy(sbuf.at[m, 0], o_in.at[m])

    def weight_grad(g, left, rights):
        def body(c, carry):
            lanes = pl.ds(pl.multiple_of(c * cols, cols), cols)
            for lo, hi, right in rights:
                total = tn(left[0, :, lanes], right[0])
                for m in range(1, mbs):
                    total = total + tn(left[m, :, lanes], right[m])
                w[g, lanes, lo:hi] = total.astype(BF16)
            return carry

        lax.fori_loop(0, width // cols, body, 0)

    def wrow(g, index):
        return w.at[g, pl.ds(pl.multiple_of(index * shard, shard), shard)]

    gsends = []

    def rs_start(g):
        for kk in range(nz):
            zz = (p.z + kk) % nz
            other = 2 * zz + 1 - p.xi
            copy = remote(wrow(g, other), xrecv.at[g, zz], xs.at[g, kk], xr.at[g, zz], dp=p.xn)
            copy.start()
            gsends.append(copy)

    def rs_mid(g):
        for kk in range(nz - 1, -1, -1):
            zz = (p.z + kk) % nz
            remote(xrecv.at[g, zz], xrecv.at[g, zz], xs.at[g, kk], xr.at[g, zz], dp=p.xn).wait_recv()
            if kk:
                mine = 2 * zz + p.xi
                xrecv[g, zz] = (
                    xrecv[g, zz].astype(F32) + rows_of(w.at[g], mine, shard).astype(F32)
                ).astype(BF16)
                copy = remote(
                    xrecv.at[g, zz], zrecv.at[g, kk - 1], zs.at[g, kk - 1], zr.at[g, kk - 1], dp=mine
                )
                copy.start()
                gsends.append(copy)

    def rs_end(g):
        total = xrecv[g, p.z].astype(F32) + rows_of(w.at[g], p.d, shard).astype(F32)
        for kk in range(1, nz):
            remote(zrecv.at[g, kk - 1], zrecv.at[g, kk - 1], zs.at[g, kk - 1], zr.at[g, kk - 1], dp=p.xn).wait_recv()
            total = total + zrecv[g, kk - 1].astype(F32)
        fin = attn.at[g // 2, pl.ds((g % 2) * shard, shard)]
        fin[...] = total
        if g == 0:
            for i, dst in enumerate((o_gq, o_gk, o_gv, o_go)):
                ocopy(fin.at[:, pl.ds(i * hw, hw)], dst)
        else:
            ocopy(fin, (o_gu, o_gg, o_gd)[g - 1])

    for copy in l_vec + [l_gm0, l_w3] + l_ug[0]:
        copy.wait()
    stage_inner(0)
    for copy in l_w12:
        copy.wait()
    stage_back(0)
    for copy in l_ug[1]:
        copy.wait()
    stage_inner(1)
    stage_back(1)
    for copy in l_inner + l_rows + l_hid:
        copy.wait()
    stage_attn(0)
    weight_grad(3, gm, [(0, hidden, inner)])
    rs_start(3)
    gg.drain()
    l_mid = [lcopy(i_mid.at[m], gm.at[m]) for m in range(mbs)]
    stage_attn(1)
    for copy in l_mid:
        copy.wait()
    weight_grad(1, gm, [(0, hidden, up)])
    rs_start(1)
    l_x = [lcopy(i_x.at[m], up.at[m]) for m in range(mbs)]
    for copy in [l_w0] + l_tab + l_att[0] + l_att[1]:
        copy.wait()
    stage_mixed(0)
    attend(0)
    rs_mid(3)
    stage_in(0)
    stage_mixed(1)
    weight_grad(2, gm, [(0, hidden, gate)])
    rs_start(2)
    rs_mid(1)
    attend(1)
    stage_in(1)
    rs_mid(2)
    for copy in l_x:
        copy.wait()
    weight_grad(0, up, [(0, hw, q), (hw, 2 * hw, k), (2 * hw, 3 * hw, v)])
    weight_grad(0, ga, [(3 * hw, 4 * hw, mixed)])
    rs_start(0)

    per = width // 128
    for r in range(5):
        sums = jnp.sum(acc[8 * r : 8 * r + 8, :], axis=0, keepdims=True)
        for j in range(per):
            vsend[per * r + j : per * r + j + 1, :] = sums[:, 128 * j : 128 * j + 128]
    vcopies = []
    for i, peer in enumerate(p.dpeers):
        copy = remote(vsend, vrecv.at[i], vs.at[i], vr.at[i], dp=peer)
        copy.start()
        vcopies.append(copy)
    stage_out(0)
    stage_out(1)
    rs_end(3)
    rs_end(1)
    total = vsend[...]
    for i in range(n - 1):
        remote(vrecv.at[i], vrecv.at[i], vs.at[i], vr.at[i], dp=p.xn).wait_recv()
        total = total + vrecv[i]
    tv[p.t] = total
    for i, peer in enumerate(p.tpeers):
        copy = remote(tv.at[p.t], tv.at[p.t], vs.at[n - 1 + i], vr.at[n - 1 + i], tensor=peer)
        copy.start()
        vcopies.append(copy)
    rs_mid(0)
    rs_end(2)
    for i, peer in enumerate(p.tpeers):
        src = (p.t + 4 - (i + 1)) % 4
        remote(tv.at[src], tv.at[src], vs.at[n - 1 + i], vr.at[n - 1 + i], tensor=peer).wait_recv()
    ocopy(tv, o_tv)
    rs_end(0)
    for gather in gga:
        gather.drain()
    for copy in gsends + vcopies:
        copy.wait_send()
    for copy in outs:
        copy.wait()


def shards(
    hidden_in, out_grad, doc_ids, w_query, w_key, w_value, w_output, w_up, w_gate, w_down,
    scale_qk, alpha_attn, alpha_mlp, scale_up, scale_gate,
):
    n = lax.axis_size("dp")
    mbs, rows, width = hidden_in.shape
    seq = doc_ids.shape[2]
    hw = w_query.shape[1]
    hidden = w_up.shape[1]
    shard = w_query.shape[0]
    nz = n // 2
    flat = 4 * lax.axis_index("dp") + lax.axis_index("tensor")

    wsh = jnp.stack(
        [
            jnp.concatenate([w_query, w_key, w_value, w_output.T], axis=1),
            w_up,
            w_gate,
            w_down.T,
        ]
    )

    def placed(vals):
        start = (flat * vals.shape[0]) % 128
        return lax.dynamic_update_slice(jnp.zeros((128,), F32), vals, (start,))

    zero = jnp.zeros((128,), F32)
    small = jnp.stack(
        [placed(item) for item in (scale_qk, alpha_attn, alpha_mlp, scale_up, scale_gate)] + [zero] * 3
    )
    docs = doc_ids[:, 0, :]
    places = doc_places(docs)
    steps = jnp.arange(DH // 2, dtype=F32) / (DH // 2)
    freqs = jnp.exp(-math.log(10000.0) * steps)
    turn = places.astype(F32)[..., None] * freqs
    cosine, sine = jnp.cos(turn), jnp.sin(turn)
    code = (docs * CODE + places // BLOCK).astype(F32)
    low = (docs * CODE).astype(F32)
    table = jnp.concatenate(
        [cosine, sine, code[..., None], low[..., None], jnp.zeros(code.shape + (126 - DH,), F32)], axis=-1
    )
    irow = jnp.stack([code, low] + [code] * 6, axis=1)

    any_ = pl.BlockSpec(memory_space=pl.ANY)
    vm = pltpu.VMEM
    dma = pltpu.SemaphoreType.DMA

    def sds(shape, dtype):
        return jax.ShapeDtypeStruct(shape, dtype)

    res_shapes = dict(
        out=((mbs, rows, width), BF16),
        w=((4, width, width), BF16),
        x=((mbs, seq, width), BF16),
        q=((mbs, seq, hw), BF16),
        k=((mbs, seq, hw), BF16),
        v=((mbs, seq, hw), BF16),
        rq=((mbs, seq, hw), BF16),
        rk=((mbs, seq, hw), BF16),
        lrow=((mbs, seq // 16, 128), F32),
        mixed=((mbs, seq, hw), BF16),
        mid=((mbs, seq, width), BF16),
        up=((mbs, seq, hidden), BF16),
        gate=((mbs, seq, hidden), BF16),
        inner=((mbs, seq, hidden), BF16),
        attn=((mbs, rows, width), F32),
        gmd=((mbs, rows, width), F32),
        gm=((mbs, rows, width), BF16),
        gm0=((seq, width), BF16),
        vec=((8, width), F32),
        acc=((40, width), F32),
    )
    r = {key: sds(*val) for key, val in res_shapes.items()}
    s = {key: vm(*val) for key, val in res_shapes.items()}
    tabs = [vm((mbs, seq, 128), F32)]
    infos = [vm((mbs, 8, seq), F32)]
    nvec = 5 * (width // 128)
    own32 = vm((mbs, rows, width), F32)
    scat = [vm((mbs, 3, rows, width), BF16), vm((mbs, 3, rows, width), BF16)]
    heads = hw // DH
    res = pl.pallas_call(
        functools.partial(fwd_kernel, n),
        name="fwd",
        out_shape=tuple(r.values()),
        in_specs=[any_] * 6,
        out_specs=tuple([any_] * len(r)),
        scratch_shapes=[
            s["w"], s["x"], s["q"], s["k"], s["v"], s["rq"], s["rk"],
            vm((mbs, seq, 128), F32),
            s["mixed"], s["mid"], s["up"], s["gate"], s["inner"],
            s["attn"], own32, own32, s["gmd"], s["gm"], s["gm0"], s["vec"], s["acc"],
            vm((4 * n, 8, 128), F32),
            *tabs,
            vm((mbs, rows, width), BF16), vm((mbs, rows, width), BF16),
            *infos,
            vm((heads * QB, hw), BF16),
            *scat,
            dma((4, n)), dma((4, n)), dma((4,)),
            dma((n + 2,)), dma((n + 2,)),
            dma((16,)),
            dma((mbs, 3)), dma((mbs, 3)), dma((mbs, 3)), dma((mbs, 3)), dma((3,)), dma((3,)),
            dma((mbs, 3)), dma((mbs, 3)), dma((mbs, 3)), dma((mbs, 3)),
            dma((40,)),
        ],
        compiler_params=pltpu.CompilerParams(
            collective_id=0, has_side_effects=True, vmem_limit_bytes=VMEM_LIMIT
        ),
    )(wsh, hidden_in, out_grad, small, table, irow)
    r = dict(zip(r, res))

    gshape = sds((shard, hw), F32)
    fshape = sds((shard, hidden), F32)
    grads = pl.pallas_call(
        functools.partial(bwd_kernel, n),
        name="bwd",
        out_shape=(
            sds((mbs, rows, width), BF16), gshape, gshape, gshape, gshape, fshape, fshape, fshape,
            sds((4, nvec, 128), F32),
        ),
        in_specs=[any_] * 22,
        out_specs=tuple([any_] * 9),
        scratch_shapes=[
            s["w"], s["q"], s["k"], s["v"], s["rq"], s["rk"], s["lrow"], s["mixed"],
            s["up"], s["gate"], s["inner"], s["attn"], s["gmd"],
            s["x"], s["x"], s["vec"], s["acc"],
            *tabs, *infos,
            vm((hw, seq), BF16), vm((hw, seq), F32), vm((seq, hw), F32), vm((seq, hw), F32),
            own32,
            vm((4, nz, shard, width), BF16), vm((4, nz - 1, shard, width), BF16),
            vm((nvec, 128), F32), vm((n - 1, nvec, 128), F32), vm((4, nvec, 128), F32),
            *scat,
            dma((48,)), dma((3,)), dma((3,)), dma((mbs, 3)), dma((mbs, 3)),
            dma((mbs, 3)), dma((mbs, 3)), dma((mbs, 3)), dma((mbs, 3)),
            dma((4, nz)), dma((4, nz)), dma((4, nz - 1)), dma((4, nz - 1)),
            dma((n + 2,)), dma((n + 2,)),
            dma((16,)),
        ],
        compiler_params=pltpu.CompilerParams(
            collective_id=1, has_side_effects=True, vmem_limit_bytes=VMEM_LIMIT
        ),
    )(
        hidden_in, table, irow, r["w"], r["x"], r["q"], r["k"], r["v"], r["rq"], r["rk"], r["lrow"],
        r["mixed"], r["mid"], r["up"], r["gate"], r["inner"], r["attn"], r["gmd"], r["gm"], r["gm0"],
        r["vec"], r["acc"],
    )
    g_in, gq, gk, gv, go, gu, gg, gd, tv = grads
    tv = tv.reshape(4, 5, width)
    total = jnp.sum(tv, axis=0)

    def own_part(flat_vals, size):
        return lax.dynamic_slice_in_dim(flat_vals, flat * size, size)

    one = scale_qk.shape[0]
    big = scale_up.shape[0]
    return (
        r["out"], g_in, gq, gk, gv, go.T, gu, gg, gd.T,
        own_part(tv[:, 4, :hw].reshape(-1), one),
        own_part(total[1], one),
        own_part(total[0], one),
        own_part(tv[:, 2, :].reshape(-1), big),
        own_part(tv[:, 3, :].reshape(-1), big),
    )


def solution(mesh):
    rows = P("dp", "tensor", None)
    inward = P("dp", "tensor")
    outward = P("tensor", "dp")
    flat = P(("dp", "tensor"))
    weights = (inward, inward, inward, outward, inward, inward, outward)
    in_specs = (rows, rows, P("dp", None, None)) + weights + (flat,) * 5
    out_specs = (rows, rows) + weights + (flat,) * 5
    return jax.shard_map(shards, mesh=mesh, in_specs=in_specs, out_specs=out_specs, check_vma=False)
```

time: 1390 us -> 460 us (0.33)
  waiting for transfers between devices: 754 us -> 0 us
  Pallas kernels: 0 us -> 413 us
  blocking collectives: 286 us -> 0 us
  matrix products: 203 us -> 0 us
  other arithmetic: 82.1 us -> 9.6 us
  between operations: 18.2 us -> 1.22 us
    reduce_scatter x15 -> x0, waiting for transfers between devices: 633 us -> none  [the longest x8 215 us: scattered(): lax.psum_scatter(sent, axis, scatter_dimension=0, tiled=True)]
    pallas_call x0 -> x2, Pallas kernels: none -> 413 us  [the longest x1 234 us: shards(): pl.pallas_call(functools.partial(fwd_kernel, n), name='fwd', out_shape=tu...]
    dot_general x66 -> x0, matrix products: 203 us -> none  [the longest x4 24.5 us: attend_backward(): jnp.einsum('qhd,khd->hqk', grad_rows, values, preferred_element_type=jnp....]
    all_gather x6 -> x0, blocking collectives: 203 us -> none  [the longest x1 40.8 us: shards(): lax.all_gather(scale_up, ('dp', 'tensor'), axis=0, tiled=True)]
    all_gather x11 -> x0, waiting for transfers between devices: 118 us -> none  [the longest x1 42.3 us: shards(): lax.all_gather(w_down, 'dp', axis=1, tiled=True)]
    unnamed x2 -> x0, blocking collectives: 83.2 us -> none
    reduce_sum x21 -> x1, other arithmetic: 36.9 us -> 1.05 us  [shards(): total = jnp.sum(tv, axis=0)]
    convert_element_type x17 -> x3, other arithmetic: 28.8 us -> 1.51 us  [the longest x1 0.75 us: shards(): low = (docs * CODE).astype(F32)]
  transfers between devices with their start and end apart: 26 -> 0, of which waited for: 20 -> 0; matrix products, arithmetic and copies ran while one was open for 13% -> 0% of each run, Pallas kernels for 0% -> 0%
where the time goes in v1:
time: 460 us; the launch traced here: 452 us
  Pallas kernels  413 us (90%)
  local copies, waits for them, and re-layouts  27.9 us (6%)
  other arithmetic  9.6 us (2%)
    pallas_call x1, Pallas kernels, shards(): pl.pallas_call(functools.partial(fwd_kernel, n), name='fwd', out_shape=tu...  234 us
    pallas_call x1, Pallas kernels, shards(): pl.pallas_call(functools.partial(bwd_kernel, n), name='bwd', out_shape=(s...  179 us
    unnamed x24, local copies, waits for them, and re-layouts  13.2 us

profile of v1, /device:TPU:0, one launch (start us, length us, event | category | flops | bytes accessed | tf_op | source)
XLA Modules:
  0.0 451.5 jit_solution(11215243003125542092)
XLA Ops:
  0.7 0.8 dynamic_update_slice.16
  1.5 0.8 dynamic_update_slice.15
  2.2 0.8 dynamic_update_slice.14
  3.0 1.3 stack.61.small
  4.3 0.7 copy.55
  5.0 0.2 convert_reduce_fusion
  5.2 0.1 select_reduce_fusion
  5.3 0.8 fusion
  6.1 0.8 fusion.1
  6.8 0.7 stack.62.irow
  7.5 0.9 copy.47
  8.5 0.9 maximum_bitcast_fusion
  9.4 1.1 copy.48
  10.5 2.1 pad_maximum_fusion.wsh
  12.6 0.4 copy.49
  13.0 1.4 copy.50
  14.4 3.7 multiply_sine_fusion
  18.1 1.0 broadcast_in_dim.2
  19.1 4.3 concatenate.7.table
  23.4 234.1 %fwd.1 = (bf16[2,256,1024]{2,1,0:T(8,128)(2,1)}, bf16[4,1024,1024]{2,1,0:T(8,128)(2,1)}, bf16[2,1024,1024]{2,1,0:T(8,128)(2,1)}, bf16[2,1024,256]{2,1,0:T(8,128)...) custom-call(bf16[4,128,1024]{2,1,0:T(8,128)(2,1)} %pad_maximum_fusio, ...), custom_call_target="tpu_custom_call" | custom-call | tf_op jit(solution)/shard_map/fwd/pallas_call | solution.py:955
  257.5 178.7 %bwd.1 = (bf16[2,256,1024]{2,1,0:T(8,128)(2,1)}, f32[128,256]{1,0:T(8,128)}, f32[128,256]{1,0:T(8,128)}, f32[128,256]{1,0:T(8,128)}, f32[128,256]{1,0:T(8,128)},...) custom-call(bf16[2,256,1024]{2,1,0:T(8,128)(2,1)} %hid.3, ...), custom_call_target="tpu_custom_call" | custom-call | tf_op jit(solution)/shard_map/bwd/pallas_call | solution.py:987
  436.2 0.0 copy-start
  436.2 0.0 copy-start.5
  436.3 0.0 copy-start.4
  436.3 0.0 copy-start.3
  436.3 0.0 copy-start.2
  436.3 0.0 copy-start.1
  436.3 1.0 reduce_sum.35
  437.4 0.6 dynamic-slice_bitcast_fusion
  437.9 0.9 reshape.205
  438.9 0.6 dynamic_slice.25
  439.5 0.6 dynamic_slice.24
  440.1 0.6 dynamic_slice.19
  440.7 1.7 copy.51
  442.3 2.0 copy.52
  444.4 2.3 copy.67
  446.6 0.0 copy-done
  446.6 1.0 copy.68
  447.6 0.0 copy-done.5
  447.6 0.7 copy.69
  448.2 0.0 copy-done.4
  448.2 0.7 copy.70
  448.9 0.0 copy-done.3
  448.9 0.7 copy.71
  449.6 0.0 copy-done.2
  449.6 0.8 copy.72
  450.4 0.0 copy-done.1
  450.4 0.8 copy.73
  (12 shorter events, 0.1 us)
Async XLA Ops:
  436.2 10.4 %copy-start = (bf16[2,256,1024]{2,1,0:T(8,128)(2,1)S(1)}, bf16[2,256,1024]{2,1,0:T(8,128)(2,1)}, u32[]{:S(2)}) copy-start(bf16[2,256,1024]{2,1,0:T(8,128)(2,1)} %get-tuple-element.140) | copy-start | bytes 3145732
  436.2 11.3 %copy-start.5 = (f32[128,256]{1,0:T(8,128)S(1)}, f32[128,256]{1,0:T(8,128)}, u32[]{:S(2)}) copy-start(f32[128,256]{1,0:T(8,128)} %get-tuple-element.141) | copy-start | bytes 393220
  436.3 12.0 %copy-start.4 = (f32[128,256]{1,0:T(8,128)S(1)}, f32[128,256]{1,0:T(8,128)}, u32[]{:S(2)}) copy-start(f32[128,256]{1,0:T(8,128)} %get-tuple-element.142) | copy-start | bytes 393220
  436.3 12.6 %copy-start.3 = (f32[128,256]{1,0:T(8,128)S(1)}, f32[128,256]{1,0:T(8,128)}, u32[]{:S(2)}) copy-start(f32[128,256]{1,0:T(8,128)} %get-tuple-element.143) | copy-start | bytes 393220
  436.3 13.3 %copy-start.2 = (f32[128,1024]{1,0:T(8,128)S(1)}, f32[128,1024]{1,0:T(8,128)}, u32[]{:S(2)}) copy-start(f32[128,1024]{1,0:T(8,128)} %get-tuple-element.145) | copy-start | bytes 1572868
  436.3 14.1 %copy-start.1 = (f32[128,1024]{1,0:T(8,128)S(1)}, f32[128,1024]{1,0:T(8,128)}, u32[]{:S(2)}) copy-start(f32[128,1024]{1,0:T(8,128)} %get-tuple-element.146) | copy-start | bytes 1572868
